TPU v7x, 128 devices: a whole 4x4x4 slice. The times are simulated.
128 devices in a mesh: gen: 4 (over z), learn: 32 (over x, y, core).
Axes of the slice: x: 4, y: 4, z: 4, core: 2. Of those that a mesh axis runs over, the one named last changes fastest.
Arguments:
- hidden: bfloat16 [32768, 5120], P(('gen', 'learn')), may hold values from -0.59765625 to 0.59765625
- cotangent: bfloat16 [32768, 1024], P(('gen', 'learn')), may hold values from -0.29882812 to 0.29882812
- importance: float32 [32768], P(('gen', 'learn')), may hold values from 0.25 to 4
- block_len: int32 [4096], P(('gen', 'learn')), may hold values from 1 to 8
- version: int32 [4096], P(('gen', 'learn')), may hold values from 0 to 3
- destination: int32 [4096, 1], P(('gen', 'learn')), may hold values from 0 to 31; in each aligned block of 32 rows (0 to 31, 32 to 63, ...) at most 2 rows name the same one
- w_key: bfloat16 [5120, 1024], replicated, may hold values from -0.078125 to 0.078125
- in_gain: float32 [5120], replicated, may hold values from 0.5 to 1.5
- key_gain: float32 [128], replicated, may hold values from 0.5 to 1.5
Outputs:
- grad_slots: bfloat16 [65536, 5120], P(('gen', 'learn'))
- w_grad: float32 [5120, 1024], P('gen')
- gain_grad: float32 [5120], replicated
- kgain_grad: float32 [128], replicated
Inputs may be any that keep to these rules, and one draw needn't show every extreme that they name: `destination`: the 32 blocks of one device name each learner at most 2 times.
All inputs are finite; a program needn't handle non-finite values.
Results may differ from a plain program's by a relative error of at most 0.0075.
Values may be sent and summed in bfloat16 or wider, within the bound.
A program may use at most 128 MiB of HBM per device.

v0:
```python
import jax
import jax.numpy as jnp
from jax import lax
from jax.sharding import PartitionSpec as P

TILE = 8
VERSIONS = 4
SLOTS = 64
epsilon = 1e-06
clip_ratio = 2.0
staleness = 0.5


def packed_total(arrays, axis):
    ends = [0]
    for a in arrays:
        ends.append(ends[-1] + a.size)
    so_far = lax.psum(jnp.concatenate([a.ravel() for a in arrays]), axis)
    return tuple((so_far[b:e].reshape(a.shape) for a, b, e in zip(arrays, ends, ends[1:])))


def token_weights(importance, block_len, version):
    tile_count = block_len.shape[0]
    inside = (lax.broadcasted_iota(jnp.int32, (tile_count, TILE), 1) < block_len[:, None]).astype(
        jnp.float32
    )
    stale_age = (VERSIONS - 1 - version).astype(jnp.float32)
    decay_factor = jnp.power(jnp.float32(staleness), stale_age)
    return jnp.minimum(importance, clip_ratio) * (decay_factor[:, None] * inside).reshape(-1)


def layer_pass(hidden, upstream_rows, w_key, in_gain, key_gain):
    row_count = hidden.shape[0]
    x_float = hidden.astype(jnp.float32)
    inv_rms = lax.rsqrt(jnp.mean(x_float * x_float, -1, keepdims=True) + epsilon)
    normed = x_float * inv_rms
    h_rows = (normed * in_gain).astype(jnp.bfloat16)
    key_rows = jnp.dot(h_rows, w_key, preferred_element_type=jnp.float32).reshape(
        row_count, -1, key_gain.shape[0]
    )
    key_scale = lax.rsqrt(jnp.mean(key_rows * key_rows, -1, keepdims=True) + epsilon)
    upstream = upstream_rows.astype(jnp.float32).reshape(key_rows.shape)
    kgain_part = jnp.sum(upstream * key_rows * key_scale, axis=(0, 1))
    scaled = upstream * key_gain
    grad_keys = key_scale * scaled - key_rows * key_scale**3 * jnp.mean(
        scaled * key_rows, -1, keepdims=True
    )
    grad_keys = grad_keys.reshape(row_count, -1).astype(jnp.bfloat16)
    grad_h = lax.dot_general(
        grad_keys, w_key, (((1,), (1,)), ((), ())), preferred_element_type=jnp.float32
    )
    gain_part = jnp.sum(grad_h * normed, 0)
    grad_normed = grad_h * in_gain
    grad_input = inv_rms * (
        grad_normed - normed * jnp.mean(grad_normed * normed, -1, keepdims=True)
    )
    return (grad_input.astype(jnp.bfloat16), h_rows, grad_keys, gain_part, kgain_part)


def body(hidden, cotangent, importance, block_len, version, destination, w_key, in_gain, key_gain):
    learners = lax.axis_size("learn")
    generators = lax.axis_size("gen")
    capacity = SLOTS // learners
    tile_count = block_len.shape[0]
    model_width = hidden.shape[1]
    weights = token_weights(importance, block_len, version)
    upstream_all = (cotangent.astype(jnp.float32) * weights[:, None]).astype(jnp.bfloat16)
    dest_column = destination[:, 0]
    onehot = (dest_column[:, None] == jnp.arange(learners, dtype=jnp.int32)[None, :]).astype(
        jnp.int32
    )
    slot_rank = jnp.sum((jnp.cumsum(onehot, 0) - onehot) * onehot, 1)
    target = dest_column * capacity + slot_rank
    placing = (target[None, :] == jnp.arange(SLOTS, dtype=jnp.int32)[:, None]).astype(jnp.bfloat16)
    grad_local, h_rows, grad_keys, gain_part, kgain_part = layer_pass(
        hidden, upstream_all, w_key, in_gain, key_gain
    )
    feature_count = grad_local.shape[1]
    spread = jnp.dot(
        placing,
        grad_local.reshape(tile_count, TILE * feature_count),
        preferred_element_type=jnp.float32,
    )
    grad_slots = lax.all_to_all(
        spread.astype(jnp.bfloat16).reshape(SLOTS * TILE, feature_count),
        "learn",
        split_axis=0,
        concat_axis=0,
        tiled=True,
    )
    row_count = h_rows.shape[0]
    group_width = model_width // generators
    sliced = h_rows.reshape(row_count, generators, group_width)
    arrived_rows = lax.all_to_all(sliced, "gen", split_axis=1, concat_axis=0, tiled=True).reshape(
        generators * row_count, group_width
    )
    gathered_keys = lax.all_gather(grad_keys, "gen", axis=0, tiled=True)
    partial_rows = lax.dot_general(
        arrived_rows, gathered_keys, (((0,), (0,)), ((), ())), preferred_element_type=jnp.float32
    )
    w_grad = lax.psum(partial_rows, "learn")
    gain_grad, kgain_grad = packed_total((gain_part, kgain_part), ("gen", "learn"))
    return (grad_slots, w_grad, gain_grad, kgain_grad)


def solution(mesh):
    return jax.shard_map(
        body,
        mesh=mesh,
        in_specs=(
            P(("gen", "learn"), None),
            P(("gen", "learn"), None),
            P(("gen", "learn")),
            P(("gen", "learn")),
            P(("gen", "learn")),
            P(("gen", "learn"), None),
            P(),
            P(),
            P(),
        ),
        out_specs=(P(("gen", "learn"), None), P("gen", None), P(), P()),
        check_vma=False,
    )
```

profile of v0, /device:TPU:1, one launch (start us, length us, event | category | flops | bytes accessed | tf_op | source)
XLA Modules:
  0.0 262.8 jit_solution(8460036367396275193)
XLA Ops:
  7.2 0.0 all-gather.2.cloned.1.call-start
  7.2 2.3 fusion.10
  9.6 2.5 fusion.4
  12.1 0.0 copy-start.1
  12.1 0.0 copy-start.10
  12.1 0.0 copy-start.9
  12.1 0.0 copy-start.8
  12.1 0.0 copy-start.4
  12.1 6.5 %fusion.19 = f32[256,1024]{1,0:T(8,128)S(1)} fusion(bf16[256,5120]{1,0:T(8,128)(2,1)S(1)} %fusion.4, bf16[5120,1024]{1,0:T(8,128)(2,1)} %param.15), kind=kOutput, calls=%fused_computation.47 | convolution fusion | flops 2684354560 | bytes 14155776 | tf_op jit(solution)/shard_map/dot_general | solution.py:38
  18.7 0.0 copy-done.1
  18.7 0.0 copy-start.6
  18.7 0.2 copy.26
  18.9 0.0 copy-done.10
  18.9 0.0 copy-done.9
  19.0 0.1 fusion.18
  19.0 0.1 mul.159
  19.1 0.0 copy-done.8
  19.1 0.0 copy-done.4
  19.1 0.1 convert_bitcast_fusion
  19.3 0.2 copy.29
  19.5 0.0 copy-done.6
  19.5 0.1 bitcast_multiply_fusion.1
  19.6 0.7 multiply_reduce_fusion.1
  20.3 0.1 copy.19
  20.4 0.1 copy.20
  20.5 0.1 copy.21
  20.7 0.1 copy.22
  20.7 0.1 copy.23
  20.9 0.3 mul.155
  21.2 0.3 mul.168
  21.5 0.3 mul.174
  21.9 1.8 fusion.15
  23.7 0.0 all-gather.2.cloned.1.call-update
  23.7 0.0 copy-start
  23.8 0.0 copy-start.3
  23.8 0.0 copy-start.5
  23.8 3.6 %copy.36 = bf16[32,4,8,1280]{3,2,0,1:T(8,128)(2,1)} copy(bf16[32,4,8,1280]{3,2,1,0:T(8,128)(2,1)} %bitcast.43) | data formatting | bytes 5242880 | tf_op jit(solution)/shard_map/reshape | solution.py:93
  27.3 5.8 %all-to-all-start.1 = ((bf16[256,4,1280]{2,0,1:T(8,128)(2,1)}), bf16[256,4,1280]{2,0,1:T(8,128)(2,1)}, u32[]{:S(2)}, u32[]{:S(2)}) async-start(bf16[256,4,1280]{2,0,1:T(8,128)(2,1)} %bitcast.44), calls=%async_computation.1 | async-start | bytes 5242880 | tf_op jit(solution)/shard_map/all_to_all | solution.py:94
  33.2 0.0 copy-done
  33.2 0.0 copy-done.3
  33.2 0.0 copy-done.5
  33.2 6.5 %fusion.9 = (f32[5120]{0:T(1024)S(1)}, f32[256]{0:T(256)S(1)}, f32[256,5120]{1,0:T(8,128)S(1)}) fusion(bf16[256,5120]{1,0:T(8,128)(2,1)S(1)} %copy-done, f32[256]{0:T(256)S(1)} %add_rsqrt_fusion.1, f32[5120]{0:T(1024)S(1)} %copy-done.5, bf16[256,1024]{1,0:T(8,128)(2,1)S(1)} %copy-done.3, bf16[5120,1024]{1,0:T(8,128)(2,1)} %param.15), kind=kOutput, calls=%fused_computation.12 | convolution fusion | flops 2693524224 | bytes 18917376 | tf_op jit(solution)/shard_map/dot_general | solution.py:49
  39.7 3.0 %fusion.8 = bf16[256,5120]{1,0:T(8,128)(2,1)} fusion(bf16[256,5120]{1,0:T(8,128)(2,1)S(1)} %copy-done, f32[256,5120]{1,0:T(8,128)S(1)} %get-tuple-element.12, f32[256]{0:T(256)S(1)} %broadcast_multiply_fusion.1, f32[5120]{0:T(1024)S(1)} %copy-done.5, f32[256]{0:T(256)S(1)} %add_rsqrt_fusion.1), kind=kLoop, calls=%fused_computation.11 | loop fusion | flops 9175040 | bytes 10508288 | tf_op jit(solution)/shard_map/convert_element_type | solution.py:57
  42.7 3.2 %reshape.87 = bf16[32,40960]{1,0:T(8,128)(2,1)S(1)} reshape(bf16[256,5120]{1,0:T(8,128)(2,1)} %fusion.8) | data formatting | bytes 5242880 | tf_op jit(solution)/shard_map/reshape | solution.py:81
  45.9 0.0 copy-done.7
  45.9 0.1 fusion.17
  46.0 0.1 reduce_window_sum.11
  46.0 0.2 select_reduce_fusion
  46.2 3.9 %convolution_convert_fusion = bf16[64,40960]{1,0:T(8,128)(2,1)} fusion(bf16[32,40960]{1,0:T(8,128)(2,1)S(1)} %reshape.87, s32[32]{0:T(128)S(1)} %multiply_add_fusion), kind=kOutput, calls=%fused_computation | convolution fusion | flops 170395648 | bytes 7864448 | tf_op jit(solution)/shard_map/dot_general | solution.py:79
  50.1 8.1 %all_to_all.19 = bf16[32,16,5120]{2,1,0:T(8,128)(2,1)} reshape(bf16[64,40960]{1,0:T(8,128)(2,1)} %convolution_convert_fusion) | data formatting | bytes 10485760 | tf_op jit(solution)/shard_map/all_to_all | solution.py:84
  58.2 23.3 %all-to-all-done.1 = bf16[256,4,1280]{2,0,1:T(8,128)(2,1)} async-done(((bf16[256,4,1280]{2,0,1:T(8,128)(2,1)}), bf16[256,4,1280]{2,0,1:T(8,128)(2,1)}, u32[]{:S(2)}, u32[]{:S(2)}) %all-to-all-start.1) | async-done | bytes 2621472 | tf_op jit(solution)/shard_map/all_to_all | solution.py:94
  81.5 8.8 %all-to-all-start = ((bf16[32,16,5120]{2,1,0:T(8,128)(2,1)}), bf16[32,16,5120]{2,1,0:T(8,128)(2,1)}, u32[]{:S(2)}, u32[]{:S(2)}) async-start(bf16[32,16,5120]{2,1,0:T(8,128)(2,1)} %all_to_all.19), calls=%async_computation | async-start | bytes 10485760 | tf_op jit(solution)/shard_map/all_to_all | solution.py:84
  90.3 0.0 all-reduce.2.cloned.1.call-start
  90.4 0.0 all-gather.2.cloned.1.call-done
  90.4 7.7 %fusion.20 = f32[1280,1024]{1,0:T(8,128)} fusion(bf16[1024,1280]{1,0:T(8,128)(2,1)} %bitcast.5, bf16[1024,1024]{1,0:T(8,128)(2,1)} %all-gather.2.cloned.1.call-done), kind=kOutput, calls=%fused_computation.48 | convolution fusion | flops 2684354560 | bytes 9961472 | tf_op jit(solution)/shard_map/dot_general | solution.py:98
  98.0 0.0 all-reduce.2.cloned.1.call-update
  98.1 120.7 %psum.15 = f32[5248]{0:T(1024)S(1)} all-reduce(f32[5248]{0:T(1024)S(1)} %pad_maximum_fusion), channel_id=1, replica_groups=mesh['gen'=4,'learn'=32] {'gen','learn'}, use_global_device_ids=true, to_apply=%region_10.11 | all-reduce | flops 5248 | bytes 41984 | tf_op jit(solution)/shard_map/psum | solution.py:18
  218.8 0.6 slice.8
  219.4 0.5 slice.9
  219.9 0.0 all-to-all-done
  219.9 28.3 %all-reduce.2.cloned.1.call-done = f32[1280,1024]{1,0:T(8,128)} async-done(((f32[1280,1024]{1,0:T(8,128)}), f32[1280,1024]{1,0:T(8,128)}) %all-reduce.2.cloned.1.call-update) | async-done | bytes 5242896 | tf_op jit(solution)/shard_map/psum | solution.py:101
  248.2 5.3 %copy.39 = bf16[512,5120]{1,0:T(8,128)(2,1)} copy(bf16[512,5120]{1,0:T(8,128)(2,1)} %bitcast.2) | data formatting | bytes 10485760
  253.6 0.0 copy-done.2
  253.6 2.4 copy.40
  (12 shorter events, 0.1 us)
Async XLA Ops:
  7.2 83.2 %all-gather.2.cloned.1.call-start = ((), (), s32[]{:S(2)}) async-start(), calls=%async_computation.2 | async-start | bytes 2621440 | tf_op jit(solution)/shard_map/all_gather | solution.py:97
  12.1 6.6 %copy-start.1 = (bf16[256,5120]{1,0:T(8,128)(2,1)}, bf16[256,5120]{1,0:T(8,128)(2,1)S(1)}, u32[]{:S(2)}) copy-start(bf16[256,5120]{1,0:T(8,128)(2,1)S(1)} %fusion.4) | copy-start | bytes 7864324
  12.1 6.8 %copy-start.10 = (s32[32]{0:T(128)S(1)}, s32[32]{0:T(128)}, u32[]{:S(2)}) copy-start(s32[32]{0:T(128)} %param.13) | copy-start | bytes 388
  12.1 6.8 %copy-start.9 = (s32[32]{0:T(128)S(1)}, s32[32]{0:T(128)}, u32[]{:S(2)}) copy-start(s32[32]{0:T(128)} %param.12) | copy-start | bytes 388
  12.1 7.0 %copy-start.8 = (f32[256]{0:T(256)S(1)}, f32[256]{0:T(256)}, u32[]{:S(2)}) copy-start(f32[256]{0:T(256)} %param.11) | copy-start | bytes 3076
  12.1 7.0 %copy-start.4 = (bf16[256,1024]{1,0:T(8,128)(2,1)S(1)}, bf16[256,1024]{1,0:T(8,128)(2,1)}, u32[]{:S(2)}) copy-start(bf16[256,1024]{1,0:T(8,128)(2,1)} %param.10) | copy-start | bytes 1572868
  18.7 0.8 copy-start.6
  23.7 9.4 %copy-start = (bf16[256,5120]{1,0:T(8,128)(2,1)S(1)}, bf16[256,5120]{1,0:T(8,128)(2,1)}, u32[]{:S(2)}) copy-start(bf16[256,5120]{1,0:T(8,128)(2,1)} %param.9) | copy-start | bytes 7864324
  23.8 9.4 %copy-start.3 = (bf16[256,1024]{1,0:T(8,128)(2,1)S(1)}, bf16[256,1024]{1,0:T(8,128)(2,1)}, u32[]{:S(2)}) copy-start(bf16[256,1024]{1,0:T(8,128)(2,1)} %get-tuple-element.9) | copy-start | bytes 1572868
  23.8 9.4 %copy-start.5 = (f32[5120]{0:T(1024)S(1)}, f32[5120]{0:T(1024)}, u32[]{:S(2)}) copy-start(f32[5120]{0:T(1024)} %param.16) | copy-start | bytes 61444
  27.3 54.1 %all-to-all-start.1 = ((bf16[256,4,1280]{2,0,1:T(8,128)(2,1)}), bf16[256,4,1280]{2,0,1:T(8,128)(2,1)}, u32[]{:S(2)}, u32[]{:S(2)}) async-start(bf16[256,4,1280]{2,0,1:T(8,128)(2,1)} %bitcast.44), calls=%async_computation.1 | async-start | bytes 5242880 | tf_op jit(solution)/shard_map/all_to_all | solution.py:94
  42.7 3.2 %copy-start.7 = (s32[32,1]{0,1:T(1,128)S(1)}, s32[32,1]{0,1:T(1,128)}, u32[]{:S(2)}) copy-start(s32[32,1]{0,1:T(1,128)} %param.14) | copy-start | bytes 388
  81.5 138.5 %all-to-all-start = ((bf16[32,16,5120]{2,1,0:T(8,128)(2,1)}), bf16[32,16,5120]{2,1,0:T(8,128)(2,1)}, u32[]{:S(2)}, u32[]{:S(2)}) async-start(bf16[32,16,5120]{2,1,0:T(8,128)(2,1)} %all_to_all.19), calls=%async_computation | async-start | bytes 10485760 | tf_op jit(solution)/shard_map/all_to_all | solution.py:84
  90.3 157.9 %all-reduce.2.cloned.1.call-start = ((), (), s32[]{:S(2)}) async-start(), calls=%async_computation.3 | async-start | bytes 10485760 | tf_op jit(solution)/shard_map/psum | solution.py:101
  248.2 5.3 %copy-start.2 = (f32[1280,1024]{1,0:T(8,128)S(1)}, f32[1280,1024]{1,0:T(8,128)}, u32[]{:S(2)}) copy-start(f32[1280,1024]{1,0:T(8,128)} %all-reduce.2.cloned.1.call-done) | copy-start | bytes 15728644
Sparse Core Ops, SparseCore 0:
  23.9 59.1 all-gather.1
  98.2 149.9 all-reduce.1
where the time goes:
time: 263 us
  blocking collectives  121 us (46%)
  waiting for transfers between devices  51.6 us (20%)
  local copies, waits for them, and re-layouts  25.7 us (10%)
  matrix products  24.5 us (9%)
  starting transfers between devices  14.8 us (6%)
  between operations  14.3 us (5%)
  other arithmetic  11.1 us (4%)
    psum x1, blocking collectives, packed_total(): so_far = lax.psum(jnp.concatenate([a.ravel() for a in arrays]), axis)  121 us
    psum x1, waiting for transfers between devices, body(): w_grad = lax.psum(partial_rows, 'learn')  28.3 us
    all_to_all x1, waiting for transfers between devices, body(): lax.all_to_all(sliced, 'gen', split_axis=1, concat_axis=0, tiled=True)  23.3 us
    all_to_all x1, starting transfers between devices, body(): lax.all_to_all(spread.astype(jnp.bfloat16).reshape(SLOTS * TILE, feature_...  8.84 us
    unnamed x26, local copies, waits for them, and re-layouts  8.15 us
    all_to_all x1, local copies, waits for them, and re-layouts, body(): lax.all_to_all(spread.astype(jnp.bfloat16).reshape(SLOTS * TILE, feature_...  8.08 us
    dot_general x1, matrix products, body(): lax.dot_general(arrived_rows, gathered_keys, (((0,), (0,)), ((), ())), pr...  7.66 us
    dot_general x1, matrix products, layer_pass(): jnp.dot(h_rows, w_key, preferred_element_type=jnp.float32)  6.55 us
  transfers between devices with their start and end apart: 4, of which 2 were waited for; matrix products, arithmetic and copies ran while one was open for 11% of the time, Pallas kernels for 0%

commit v1 on v0

--- a/solution.py
+++ b/solution.py
@@ -2,6 +2,7 @@
 import jax.numpy as jnp
 from jax import lax
 from jax.sharding import PartitionSpec as P
+from jax.lax import axis_size, ppermute
 
 TILE = 8
 VERSIONS = 4
@@ -98,7 +99,21 @@
     partial_rows = lax.dot_general(
         arrived_rows, gathered_keys, (((0,), (0,)), ((), ())), preferred_element_type=jnp.float32
     )
-    w_grad = lax.psum(partial_rows, "learn")
+
+    def see_lots_all(q_in):
+        world = axis_size("learn")
+        current_value, after = (q_in, 0)
+        while 1 << after < world:
+            all_rows = ppermute(
+                current_value,
+                axis_name="learn",
+                perm=[(hop_no, hop_no ^ 1 << after) for hop_no in range(world)],
+            )
+            current_value = current_value + all_rows
+            after = after + 1
+        return current_value
+
+    w_grad = see_lots_all(partial_rows)
     gain_grad, kgain_grad = packed_total((gain_part, kgain_part), ("gen", "learn"))
     return (grad_slots, w_grad, gain_grad, kgain_grad)
 

time: 263 us -> 709 us (2.70)
  waiting for transfers between devices: 51.6 us -> 333 us
  blocking collectives: 121 us -> 263 us
  other arithmetic: 11.1 us -> 37.3 us
    ppermute x0 -> x5, waiting for transfers between devices: none -> 332 us  [see_lots_all(): ppermute(current_value, axis_name='learn', perm=[(hop_no, hop_no ^ 1 << a...]
    psum x1, blocking collectives: 121 us -> 209 us  [packed_total(): so_far = lax.psum(jnp.concatenate([a.ravel() for a in arrays]), axis)]
    all_to_all x0 -> x1, blocking collectives: none -> 53.7 us  [body(): lax.all_to_all(sliced, 'gen', split_axis=1, concat_axis=0, tiled=True)]
    psum x1 -> x0, waiting for transfers between devices: 28.3 us -> none  [body(): w_grad = lax.psum(partial_rows, 'learn')]
    add x0 -> x5, other arithmetic: none -> 23.4 us  [see_lots_all(): current_value = current_value + all_rows]
    all_to_all x1 -> x0, waiting for transfers between devices: 23.3 us -> none  [body(): lax.all_to_all(sliced, 'gen', split_axis=1, concat_axis=0, tiled=True)]
    ppermute x0 -> x5, starting transfers between devices: none -> 9.48 us  [see_lots_all(): ppermute(current_value, axis_name='learn', perm=[(hop_no, hop_no ^ 1 << a...]
  transfers between devices with their start and end apart: 4 -> 7, of which waited for: 2 -> 5; matrix products, arithmetic and copies ran while one was open for 11% -> 3% of each run, Pallas kernels for 0% -> 0%
where the time goes in v1:
time: 709 us; the launch traced here: 708 us
  waiting for transfers between devices  333 us (47%)
  blocking collectives  263 us (37%)
  other arithmetic  37.3 us (5%)
  local copies, waits for them, and re-layouts  24 us (3%)
  matrix products  18.5 us (3%)
  starting transfers between devices  18 us (3%)
  between operations  14.3 us (2%)
    ppermute x5, waiting for transfers between devices, see_lots_all(): ppermute(current_value, axis_name='learn', perm=[(hop_no, hop_no ^ 1 << a...  332 us
    psum x1, blocking collectives, packed_total(): so_far = lax.psum(jnp.concatenate([a.ravel() for a in arrays]), axis)  209 us
    all_to_all x1, blocking collectives, body(): lax.all_to_all(sliced, 'gen', split_axis=1, concat_axis=0, tiled=True)  53.7 us
    add x5, other arithmetic, see_lots_all(): current_value = current_value + all_rows  23.4 us
  transfers between devices with their start and end apart: 7, of which 5 were waited for; matrix products, arithmetic and copies ran while one was open for 3% of the time, Pallas kernels for 0%

profile of v1, /device:TPU:1, one launch (start us, length us, event | category | flops | bytes accessed | tf_op | source)
XLA Modules:
  0.0 707.9 jit_solution(10041885584375264945)
XLA Ops:
  7.2 0.0 copy-start
  7.2 0.0 copy-start.9
  7.2 0.0 copy-start.5
  7.2 0.0 all-gather.2.cloned.1.call-start
  7.2 0.8 convert_power_fusion
  8.1 2.3 fusion.10
  10.4 0.7 broadcast_bitcast_fusion
  11.1 0.7 fusion.18
  11.8 0.1 mul.159
  11.9 0.7 minimum_multiply_fusion
  12.6 1.3 convert_bitcast_fusion
  13.9 0.2 copy.29
  14.1 0.1 bitcast_multiply_fusion.1
  14.2 0.8 fusion.4
  15.0 1.7 copy-done.11
  16.7 2.9 fusion.19
  19.6 0.0 copy-start.2
  19.6 0.0 copy-start.4
  19.6 0.2 copy.26
  19.8 0.6 multiply_reduce_fusion.1
  20.5 0.1 copy-done.2
  20.6 0.1 copy.19
  20.6 0.1 copy.22
  20.7 0.1 copy.20
  20.9 0.1 copy.23
  21.0 0.1 copy.21
  21.1 0.3 mul.168
  21.5 0.3 mul.174
  21.8 0.3 mul.155
  22.2 3.1 fusion.15
  25.2 0.0 all-gather.2.cloned.1.call-update
  25.3 1.9 copy.36
  27.2 53.7 %all_to_all.27 = bf16[256,4,1280]{2,0,1:T(8,128)(2,1)} all-to-all(bf16[256,4,1280]{2,0,1:T(8,128)(2,1)S(1)} %bitcast.44), channel_id=1, replica_groups=mesh['gen'=4,'learn'=32] {'gen'}, dimensions={1} | all-to-all | bytes 5242880 | tf_op jit(solution)/shard_map/all_to_all | solution.py:95
  80.9 0.9 all-gather.2.cloned.1.call-done
  81.8 5.3 fusion.20
  87.1 1.0 collective-permute-start
  88.1 8.3 %collective-permute-done = f32[1280,1024]{1,0:T(8,128)S(1)} collective-permute-done((f32[1280,1024]{1,0:T(8,128)S(1)}, f32[1280,1024]{1,0:T(8,128)S(1)}, u32[]{:S(2)}, u32[]{:S(2)}) %collective-permute-start) | collective-permute-done | bytes 5242912 | tf_op jit(solution)/shard_map/ppermute | solution.py:107
  96.4 1.8 add.54
  98.1 1.6 collective-permute-start.1
  99.7 112.9 %collective-permute-done.1 = f32[1280,1024]{1,0:T(8,128)S(1)} collective-permute-done((f32[1280,1024]{1,0:T(8,128)S(1)}, f32[1280,1024]{1,0:T(8,128)S(1)}, u32[]{:S(2)}, u32[]{:S(2)}) %collective-permute-start.1) | collective-permute-done | bytes 5242912 | tf_op jit(solution)/shard_map/ppermute | solution.py:107
  212.6 1.8 add.55
  214.4 0.0 copy-start.6
  214.4 0.0 copy-start.8
  214.4 3.0 collective-permute-start.2
  217.4 112.0 %collective-permute-done.2 = f32[1280,1024]{1,0:T(8,128)S(1)} collective-permute-done((f32[1280,1024]{1,0:T(8,128)S(1)}, f32[1280,1024]{1,0:T(8,128)S(1)}, u32[]{:S(2)}, u32[]{:S(2)}) %collective-permute-start.2) | collective-permute-done | bytes 5242912 | tf_op jit(solution)/shard_map/ppermute | solution.py:107
  329.4 3.6 add.56
  332.9 1.2 collective-permute-start.3
  334.2 6.5 fusion.9
  340.6 3.0 fusion.8
  343.7 3.2 reshape.87
  346.9 0.1 fusion.17
  346.9 0.1 reduce_window_sum.11
  347.0 0.2 select_reduce_fusion
  347.2 98.6 %collective-permute-done.3 = f32[1280,1024]{1,0:T(8,128)} collective-permute-done((f32[1280,1024]{1,0:T(8,128)}, f32[1280,1024]{1,0:T(8,128)}, u32[]{:S(2)}, u32[]{:S(2)}) %collective-permute-start.3) | collective-permute-done | bytes 5242912 | tf_op jit(solution)/shard_map/ppermute | solution.py:107
  445.8 8.1 %add.57 = f32[1280,1024]{1,0:T(8,128)} add(f32[1280,1024]{1,0:T(8,128)} %add.56, f32[1280,1024]{1,0:T(8,128)} %collective-permute-done.3) | non-fusion elementwise | flops 1310720 | bytes 15728640 | tf_op jit(solution)/shard_map/add | solution.py:112
  453.9 2.7 collective-permute-start.4
  456.7 3.9 convolution_convert_fusion
  460.5 8.1 %all_to_all.19 = bf16[32,16,5120]{2,1,0:T(8,128)(2,1)} reshape(bf16[64,40960]{1,0:T(8,128)(2,1)} %convolution_convert_fusion) | data formatting | bytes 10485760 | tf_op jit(solution)/shard_map/all_to_all | solution.py:85
  468.6 8.5 %all-to-all-start = ((bf16[32,16,5120]{2,1,0:T(8,128)(2,1)}), bf16[32,16,5120]{2,1,0:T(8,128)(2,1)}, u32[]{:S(2)}, u32[]{:S(2)}) async-start(bf16[32,16,5120]{2,1,0:T(8,128)(2,1)} %all_to_all.19), calls=%async_computation | async-start | bytes 10485760 | tf_op jit(solution)/shard_map/all_to_all | solution.py:85
  477.1 209.5 %psum.7 = f32[5248]{0:T(1024)S(1)} all-reduce(f32[5248]{0:T(1024)S(1)} %pad_maximum_fusion), channel_id=1, replica_groups=mesh['gen'=4,'learn'=32] {'gen','learn'}, use_global_device_ids=true, to_apply=%region_9.10 | all-reduce | flops 5248 | bytes 41984 | tf_op jit(solution)/shard_map/psum | solution.py:19
  686.6 0.5 slice.9
  687.1 0.6 slice.8
  687.7 8.2 %add.58 = f32[1280,1024]{1,0:T(8,128)} add(f32[1280,1024]{1,0:T(8,128)} %add.57, f32[1280,1024]{1,0:T(8,128)} %collective-permute-done.4) | non-fusion elementwise | flops 1310720 | bytes 15728640 | tf_op jit(solution)/shard_map/add | solution.py:112
  695.9 5.2 copy.38
  (24 shorter events, 0.1 us)
Async XLA Ops:
  7.2 7.1 copy-start
  7.2 7.0 copy-start.9
  7.2 7.0 copy-start.5
  7.2 74.6 %all-gather.2.cloned.1.call-start = ((), (), s32[]{:S(2)}) async-start(), calls=%async_computation.2 | async-start | bytes 2621440 | tf_op jit(solution)/shard_map/all_gather | solution.py:98
  10.4 4.6 copy-start.7
  12.6 4.1 copy-start.11
  16.7 2.9 copy-start.1
  19.6 1.0 copy-start.2
  19.6 2.5 copy-start.4
  87.1 9.3 %collective-permute-start = (f32[1280,1024]{1,0:T(8,128)S(1)}, f32[1280,1024]{1,0:T(8,128)S(1)}, u32[]{:S(2)}, u32[]{:S(2)}) collective-permute-start(f32[1280,1024]{1,0:T(8,128)S(1)} %fusion.20), channel_id=1, source_target_pairs={{0,1},{1,0},{2,3},{3,2},{4,5},{5,4},{6,7},{7,6},{8,9},{9,8},{10,11... | collective-permute-start | bytes 15728648 | tf_op jit(solution)/shard_map/ppermute | solution.py:107
  98.1 114.5 %collective-permute-start.1 = (f32[1280,1024]{1,0:T(8,128)S(1)}, f32[1280,1024]{1,0:T(8,128)S(1)}, u32[]{:S(2)}, u32[]{:S(2)}) collective-permute-start(f32[1280,1024]{1,0:T(8,128)S(1)} %add.54), channel_id=1, source_target_pairs={{0,2},{1,3},{2,0},{3,1},{4,6},{5,7},{6,4},{7,5},{8,10},{9,11},{10,... | collective-permute-start | bytes 15728648 | tf_op jit(solution)/shard_map/ppermute | solution.py:107
  214.4 119.8 %copy-start.3 = (bf16[256,1024]{1,0:T(8,128)(2,1)S(1)}, bf16[256,1024]{1,0:T(8,128)(2,1)}, u32[]{:S(2)}) copy-start(bf16[256,1024]{1,0:T(8,128)(2,1)} %get-tuple-element.9) | copy-start | bytes 1572868
  214.4 119.8 %copy-start.6 = (f32[5120]{0:T(1024)S(1)}, f32[5120]{0:T(1024)}, u32[]{:S(2)}) copy-start(f32[5120]{0:T(1024)} %param.16) | copy-start | bytes 61444
  214.4 119.7 %copy-start.8 = (f32[256]{0:T(256)S(1)}, f32[256]{0:T(256)}, u32[]{:S(2)}) copy-start(f32[256]{0:T(256)} %copy-done.7) | copy-start | bytes 3076
  214.4 115.0 %collective-permute-start.2 = (f32[1280,1024]{1,0:T(8,128)S(1)}, f32[1280,1024]{1,0:T(8,128)S(1)}, u32[]{:S(2)}, u32[]{:S(2)}) collective-permute-start(f32[1280,1024]{1,0:T(8,128)S(1)} %add.55), channel_id=1, source_target_pairs={{0,4},{1,5},{2,6},{3,7},{4,0},{5,1},{6,2},{7,3},{8,12},{9,13},{10,... | collective-permute-start | bytes 15728648 | tf_op jit(solution)/shard_map/ppermute | solution.py:107
  332.9 112.8 %collective-permute-start.3 = (f32[1280,1024]{1,0:T(8,128)}, f32[1280,1024]{1,0:T(8,128)}, u32[]{:S(2)}, u32[]{:S(2)}) collective-permute-start(f32[1280,1024]{1,0:T(8,128)} %add.56), channel_id=1, source_target_pairs={{0,8},{1,9},{2,10},{3,11},{4,12},{5,13},{6,14},{7,15},{8,0},{9,1},... | collective-permute-start | bytes 15728648 | tf_op jit(solution)/shard_map/ppermute | solution.py:107
  343.7 3.2 copy-start.10
  453.9 233.8 %collective-permute-start.4 = (f32[1280,1024]{1,0:T(8,128)}, f32[1280,1024]{1,0:T(8,128)}, u32[]{:S(2)}, u32[]{:S(2)}) collective-permute-start(f32[1280,1024]{1,0:T(8,128)} %add.57), channel_id=1, source_target_pairs={{0,16},{1,17},{2,18},{3,19},{4,20},{5,21},{6,22},{7,23},{8,24},{9,... | collective-permute-start | bytes 15728648 | tf_op jit(solution)/shard_map/ppermute | solution.py:107
  468.6 219.1 %all-to-all-start = ((bf16[32,16,5120]{2,1,0:T(8,128)(2,1)}), bf16[32,16,5120]{2,1,0:T(8,128)(2,1)}, u32[]{:S(2)}, u32[]{:S(2)}) async-start(bf16[32,16,5120]{2,1,0:T(8,128)(2,1)} %all_to_all.19), calls=%async_computation | async-start | bytes 10485760 | tf_op jit(solution)/shard_map/all_to_all | solution.py:85
Sparse Core Ops, SparseCore 0:
  25.4 56.3 all-gather.1
